TPU v7x, 32 devices: a whole 2x2x4 slice. The times are simulated.
32 devices in a mesh: src: 16 (over z, x, core), tgt: 2 (over y).
Axes of the slice: x: 2, y: 2, z: 4, core: 2. Of those that a mesh axis runs over, the one named last changes fastest.
Arguments:
- source_embed: bfloat16 [128, 65536], P(None, 'src'), may hold values from -1 to 1
- target_embed: bfloat16 [128, 1024], P(None, 'tgt'), may hold values from -1 to 1
- source_expr: bfloat16 [128, 65536], P(None, 'src'), may hold values from -0.5390625 to 0.5390625
- target_expr: bfloat16 [128, 1024], P(None, 'tgt'), may hold values from -0.5390625 to 0.5390625
- current_plan: bfloat16 [65536, 1024], P('src', 'tgt'), as said below
- source_mass: float32 [65536], P('src'), may hold values from 0.25 to 4
- target_mass: float32 [1024], P('tgt'), may hold values from 0.25 to 4
- source_potential: float32 [65536], P('src'), may hold values from -16 to 16
- target_genes: bfloat16 [1024, 256], P('tgt'), may hold values from -6 to 6
Outputs:
- imputed: bfloat16 [65536, 256], P(('src', 'tgt'))
Inputs may be any that keep to these rules, and one draw needn't show every extreme that they name: Every entry of current_plan is positive.
All inputs are finite; a program needn't handle non-finite values.
Results may differ from a plain program's by a relative error of at most 0.014.
Values may be sent and summed in bfloat16 or wider, within the bound.
A program may use at most 64 MiB of HBM per device.

v0:
```python
import jax
import jax.numpy as jnp
from jax import lax
from jax.sharding import PartitionSpec as P

ITERS = 2


epsilon = 0.05
geometry_weight = 4.0


def joined(value, axis, join):
    pieces = jax.tree.map(lambda part: lax.all_gather(part, axis), value)
    head = jax.tree.map(lambda part: part[0], pieces)
    tail = jax.tree.map(lambda part: part[1:], pieces)
    so_far, _ = lax.scan(lambda so_far, piece: (join(so_far, piece), None), head, tail)
    return so_far


def factors(embed):
    widened = embed.astype(jnp.float32)
    squares = jnp.sum(widened * widened, axis=0)
    unit_row = jnp.ones_like(squares)
    left_factor = jnp.concatenate([squares[None, :], unit_row[None, :], -2.0 * widened], axis=0)
    right_factor = jnp.concatenate([unit_row[None, :], squares[None, :], widened], axis=0)
    return (left_factor, right_factor)


def combine_pair(earlier, later):
    maximum = jnp.maximum(earlier[0], later[0])
    return (
        maximum,
        earlier[1] * jnp.exp(earlier[0] - maximum) + later[1] * jnp.exp(later[0] - maximum),
    )


def column_logsum(scores):
    local_max = jnp.max(scores, axis=0)
    local_sum = jnp.sum(jnp.exp(scores - local_max[None, :]), axis=0)
    maximum, totals = joined((local_max, local_sum), "src", combine_pair)
    return maximum + jnp.log(totals)


def row_logsum(scores):
    local_max = jnp.max(scores, axis=1)
    local_sum = jnp.sum(jnp.exp(scores - local_max[:, None]), axis=1)
    maximum, totals = joined((local_max, local_sum), "tgt", combine_pair)
    return maximum + jnp.log(totals)


def shards(
    source_embed,
    target_embed,
    source_expr,
    target_expr,
    current_plan,
    source_mass,
    target_mass,
    source_potential,
    target_genes,
):
    highest = lax.Precision.HIGHEST
    spot_rows = source_embed.shape[1]
    spot_cols = target_embed.shape[1]
    total_pairs = float(spot_rows * lax.axis_size("src") * spot_cols * lax.axis_size("tgt"))
    left_src, right_src = factors(source_embed)
    left_tgt, right_tgt = factors(target_embed)
    projected = jnp.dot(
        current_plan.astype(jnp.float32),
        right_tgt.T,
        precision=highest,
        preferred_element_type=jnp.float32,
    )
    partial_core = jnp.dot(
        right_src, projected, precision=highest, preferred_element_type=jnp.float32
    )
    core_matrix = lax.psum(partial_core, ("src", "tgt")) / total_pairs
    geometry_right = jnp.dot(
        core_matrix, left_tgt, precision=highest, preferred_element_type=jnp.float32
    )
    geometry = lax.dot_general(
        left_src,
        geometry_right,
        (((0,), (0,)), ((), ())),
        precision=highest,
        preferred_element_type=jnp.float32,
    )
    feature = lax.dot_general(
        source_expr, target_expr, (((0,), (0,)), ((), ())), preferred_element_type=jnp.float32
    )
    cost_tile = -2.0 * (feature + geometry_weight * geometry)
    log_src = jnp.log(source_mass)
    log_tgt = jnp.log(target_mass)
    potential_src = source_potential
    potential_tgt = jnp.zeros((spot_cols,), jnp.float32)
    for iteration in range(ITERS):
        potential_tgt = epsilon * log_tgt - epsilon * column_logsum(
            (potential_src[:, None] - cost_tile) / epsilon
        )
        potential_src = epsilon * log_src - epsilon * row_logsum(
            (potential_tgt[None, :] - cost_tile) / epsilon
        )
    weights = jnp.exp(
        (potential_src[:, None] + potential_tgt[None, :] - cost_tile) / epsilon
    ).astype(jnp.bfloat16)
    row_share = spot_rows // lax.axis_size("tgt")
    row_offset = lax.axis_index("tgt") * row_share
    mass_rows = lax.dynamic_slice_in_dim(source_mass, row_offset, row_share)
    numerator = lax.psum_scatter(
        jnp.dot(weights, target_genes, preferred_element_type=jnp.float32).astype(jnp.bfloat16),
        "tgt",
        scatter_dimension=0,
        tiled=True,
    ).astype(jnp.float32)
    return (numerator / mass_rows[:, None]).astype(jnp.bfloat16)


def solution(mesh):
    return jax.shard_map(
        shards,
        mesh=mesh,
        in_specs=(
            P(None, "src"),
            P(None, "tgt"),
            P(None, "src"),
            P(None, "tgt"),
            P("src", "tgt"),
            P("src"),
            P("tgt"),
            P("src"),
            P("tgt", None),
        ),
        out_specs=P(("src", "tgt"), None),
        check_vma=False,
    )
```

profile of v0, /device:TPU:0, one launch (start us, length us, event | category | flops | bytes accessed | tf_op | source)
XLA Modules:
  0.0 319.4 jit_solution(5949856165096476949)
XLA Ops:
  8.9 1.6 broadcast_multiply_fusion
  11.9 4.3 %fusion.18 = f32[130,4096]{1,0:T(8,128)S(1)} fusion(bf16[4096,512]{1,0:T(8,128)(2,1)S(1)} %copy-done.3, f32[128,512]{1,0:T(8,128)S(1)} %convert_element_type.20, f32[1,512]{1,0:T(1,128)S(1)} %bitcast.56, f32[1,512]{1,0:T(1,128)S(1)} %broadcast.34), kind=kOutput, calls=%fused_computation.38 | convolution fusion | flops 3271690240 | bytes 6590464 | tf_op jit(solution)/shard_map/dot_general | solution.py:69
  16.2 2.8 fusion.12
  19.3 5.4 %fusion.50 = f32[4096,512]{1,0:T(8,128)} fusion(bf16[128,4096]{1,0:T(8,128)(2,1)S(1)} %copy-done, bf16[128,512]{1,0:T(8,128)(2,1)} %param.16), kind=kOutput, calls=%fused_computation.86 | convolution fusion | flops 536870912 | bytes 9568256 | tf_op jit(solution)/shard_map/dot_general | solution.py:89
  24.7 117.4 %all-reduce.2.cloned.1.call-done = f32[130,130]{1,0:T(8,128)} async-done(((f32[130,130]{1,0:T(8,128)}), f32[130,130]{1,0:T(8,128)}) %all-reduce.2.cloned.1.call-update) | async-done | bytes 67616 | tf_op jit(solution)/shard_map/psum | solution.py:78
  143.4 11.4 %fusion = (f32[512]{0:T(512)S(1)}, f32[4096,512]{1,0:T(8,128)S(1)}) fusion(f32[4096]{0:T(1024)S(1)} %copy-done.5, f32[4096,512]{1,0:T(8,128)} %fusion.50, f32[130,512]{1,0:T(8,128)S(1)} %fusion.24, f32[128,4096]{1,0:T(8,128)S(1)} %get-tuple-element.123, f32[1,4096]{1,0:T(1,128)S(1)} %broadcast.33, f32[1,4096]{1,0:T(1,128)S(1)} %bitcast.47), kind=kOutput, calls=%fused_computation.16 | convolution fusion | flops 3285204480 | bytes 19191808 | tf_op jit(solution)/shard_map/dot_general | solution.py:82
  154.8 3.2 %copy-done.1 = f32[4096,512]{1,0:T(8,128)} copy-done((f32[4096,512]{1,0:T(8,128)}, f32[4096,512]{1,0:T(8,128)S(1)}, u32[]{:S(2)}) %copy-start.1) | copy-done | bytes 8388632
  158.0 1.8 exponential_reduce_fusion.3
  159.8 22.9 %all-gather.9 = f32[16,1,512]{2,1,0:T(1,128)S(1)} all-gather(f32[1,1,512]{2,1,0:T(1,128)S(1)} %bitcast.61), channel_id=3, replica_groups=mesh['src'=16,'tgt'=2] {'src'}, dimensions={0}, use_global_device_ids=true | all-gather | bytes 34816 | tf_op jit(solution)/shard_map/all_gather | solution.py:14
  182.7 17.5 %all-gather.8 = f32[16,1,512]{2,1,0:T(1,128)S(1)} all-gather(f32[1,1,512]{2,1,0:T(1,128)S(1)} %bitcast.58), channel_id=2, replica_groups=mesh['src'=16,'tgt'=2] {'src'}, dimensions={0}, use_global_device_ids=true | all-gather | bytes 34816 | tf_op jit(solution)/shard_map/all_gather | solution.py:14
  201.1 4.4 %fusion.1 = f32[4096]{0:T(1024)S(1)} fusion(f32[4096,512]{1,0:T(8,128)} %copy-done.1, f32[512]{0:T(512)S(1)} %multiply_subtract_fusion.1), kind=kLoop, calls=%fused_computation.17 | loop fusion | flops 6287360 | bytes 8407040 | tf_op jit(solution)/shard_map/reduce_max | solution.py:46
  206.8 2.2 exponential_reduce_fusion.2
  209.0 4.4 %all-gather.2 = f32[8192]{0:T(1024)S(1)} all-gather(f32[4096]{0:T(1024)S(1)} %fusion.1), channel_id=4, replica_groups=mesh['src'=16,'tgt'=2] {'tgt'}, dimensions={0}, use_global_device_ids=true | all-gather | bytes 49152 | tf_op jit(solution)/shard_map/all_gather | solution.py:14
  213.4 4.4 %all-gather.3 = f32[8192]{0:T(1024)S(1)} all-gather(f32[4096]{0:T(1024)S(1)} %exponential_reduce_fusion.2), channel_id=5, replica_groups=mesh['src'=16,'tgt'=2] {'tgt'}, dimensions={0}, use_global_device_ids=true | all-gather | bytes 49152 | tf_op jit(solution)/shard_map/all_gather | solution.py:14
  218.8 1.8 exponential_reduce_fusion.1
  220.6 18.9 %all-gather.11 = f32[16,1,512]{2,1,0:T(1,128)S(1)} all-gather(f32[1,1,512]{2,1,0:T(1,128)S(1)} %bitcast.60), channel_id=7, replica_groups=mesh['src'=16,'tgt'=2] {'src'}, dimensions={0}, use_global_device_ids=true | all-gather | bytes 34816 | tf_op jit(solution)/shard_map/all_gather | solution.py:14
  239.5 17.7 %all-gather.10 = f32[16,1,512]{2,1,0:T(1,128)S(1)} all-gather(f32[1,1,512]{2,1,0:T(1,128)S(1)} %bitcast.59), channel_id=6, replica_groups=mesh['src'=16,'tgt'=2] {'src'}, dimensions={0}, use_global_device_ids=true | all-gather | bytes 34816 | tf_op jit(solution)/shard_map/all_gather | solution.py:14
  258.1 4.4 %fusion.3 = f32[4096]{0:T(1024)S(1)} fusion(f32[4096,512]{1,0:T(8,128)} %copy-done.1, f32[512]{0:T(512)S(1)} %multiply_subtract_fusion), kind=kLoop, calls=%fused_computation.19 | loop fusion | flops 6287360 | bytes 8407040 | tf_op jit(solution)/shard_map/reduce_max | solution.py:46
  262.5 5.1 %exponential_reduce_fusion = f32[4096]{0:T(1024)S(1)} fusion(f32[4096,512]{1,0:T(8,128)} %copy-done.1, f32[4096]{0:T(1024)S(1)} %fusion.3, f32[512]{0:T(512)S(1)} %multiply_subtract_fusion), kind=kLoop, calls=%fused_computation.7 | loop fusion | flops 8384512 | bytes 8423424 | tf_op jit(solution)/shard_map/reduce_sum | solution.py:47
  267.6 4.4 %all-gather.6 = f32[8192]{0:T(1024)S(1)} all-gather(f32[4096]{0:T(1024)S(1)} %fusion.3), channel_id=8, replica_groups=mesh['src'=16,'tgt'=2] {'tgt'}, dimensions={0}, use_global_device_ids=true | all-gather | bytes 49152 | tf_op jit(solution)/shard_map/all_gather | solution.py:14
  272.0 4.4 %all-gather.7 = f32[8192]{0:T(1024)S(1)} all-gather(f32[4096]{0:T(1024)S(1)} %exponential_reduce_fusion), channel_id=9, replica_groups=mesh['src'=16,'tgt'=2] {'tgt'}, dimensions={0}, use_global_device_ids=true | all-gather | bytes 49152 | tf_op jit(solution)/shard_map/all_gather | solution.py:14
  276.5 3.2 %convolution_convert_fusion = bf16[4096,256]{1,0:T(8,128)(2,1)} fusion(bf16[512,256]{1,0:T(8,128)(2,1)S(1)} %copy-done.7, f32[4096,512]{1,0:T(8,128)S(1)} %bitcast.41, f32[4096]{0:T(1024)S(1)} %fusion.36, f32[512]{0:T(512)S(1)} %multiply_subtract_fusion), kind=kOutput, calls=%fused_computation.20 | convolution fusion | flops 1083179008 | bytes 10766336 | tf_op jit(solution)/shard_map/dot_general | solution.py:111
  279.8 30.3 %reduce-scatter.2.cloned.1.call-done = bf16[2048,256]{1,0:T(8,128)(2,1)} async-done(((bf16[4096,256]{1,0:T(8,128)(2,1)}), bf16[2048,256]{1,0:T(8,128)(2,1)}) %reduce-scatter.2.cloned.1.call-update) | async-done | bytes 1048592 | tf_op jit(solution)/shard_map/reduce_scatter | solution.py:110
  310.1 2.5 divide_convert_fusion
  (110 shorter events, 10.3 us)
Async XLA Ops:
  6.5 12.7 %copy-start = (bf16[128,4096]{1,0:T(8,128)(2,1)S(1)}, bf16[128,4096]{1,0:T(8,128)(2,1)}, u32[]{:S(2)}) copy-start(bf16[128,4096]{1,0:T(8,128)(2,1)} %param.15) | copy-start | bytes 3145732
  6.5 135.5 %all-reduce.2.cloned.1.call-start = ((), (), s32[]{:S(2)}) async-start(), calls=%async_computation.1 | async-start | bytes 278528 | tf_op jit(solution)/shard_map/psum | solution.py:78
  6.5 5.4 %copy-start.3 = (bf16[4096,512]{1,0:T(8,128)(2,1)S(1)}, bf16[4096,512]{1,0:T(8,128)(2,1)}, u32[]{:S(2)}) copy-start(bf16[4096,512]{1,0:T(8,128)(2,1)} %param.17) | copy-start | bytes 12582916
  19.0 124.4 %copy-start.5 = (f32[4096]{0:T(1024)S(1)}, f32[4096]{0:T(1024)}, u32[]{:S(2)}) copy-start(f32[4096]{0:T(1024)} %param.20) | copy-start | bytes 49156
  19.0 291.0 %reduce-scatter.2.cloned.1.call-start = ((), (), s32[]{:S(2)}) async-start(), calls=%async_computation.2 | async-start | bytes 3145728 | tf_op jit(solution)/shard_map/reduce_scatter | solution.py:110
  154.8 3.2 %copy-start.1 = (f32[4096,512]{1,0:T(8,128)}, f32[4096,512]{1,0:T(8,128)S(1)}, u32[]{:S(2)}) copy-start(f32[4096,512]{1,0:T(8,128)S(1)} %get-tuple-element.128) | copy-start | bytes 25165828
  154.8 46.2 %copy-start.6 = (f32[512]{0:T(512)S(1)}, f32[512]{0:T(512)}, u32[]{:S(2)}) copy-start(f32[512]{0:T(512)} %param.19) | copy-start | bytes 6148
  201.0 5.8 %copy-start.2 = (f32[4096,512]{1,0:T(8,128)S(1)}, f32[4096,512]{1,0:T(8,128)}, u32[]{:S(2)}) copy-start(f32[4096,512]{1,0:T(8,128)} %copy-done.1) | copy-start | bytes 25165828
  201.0 16.8 %copy-start.4 = (f32[4096]{0:T(1024)S(1)}, f32[4096]{0:T(1024)}, u32[]{:S(2)}) copy-start(f32[4096]{0:T(1024)} %param.18) | copy-start | bytes 49156
  258.1 18.4 %slice-start = ((s8[8388608]{0:T(1024)(128)(4,1)}), s8[4194304]{0:T(1024)(128)(4,1)S(1)}, s32[]{:S(2)}) async-start(s8[8388608]{0:T(1024)(128)(4,1)} %bitcast.40), calls=%async_computation.3 | async-start | bytes 8388608
  258.1 18.4 %copy-start.7 = (bf16[512,256]{1,0:T(8,128)(2,1)S(1)}, bf16[512,256]{1,0:T(8,128)(2,1)}, u32[]{:S(2)}) copy-start(bf16[512,256]{1,0:T(8,128)(2,1)} %param.21) | copy-start | bytes 786436
  262.5 14.0 %slice-start.1 = ((s8[8388608]{0:T(1024)(128)(4,1)}), s8[4194304]{0:T(1024)(128)(4,1)S(1)}, s32[]{:S(2)}) async-start(s8[8388608]{0:T(1024)(128)(4,1)} %bitcast.40), calls=%async_computation.4 | async-start | bytes 8388608
Sparse Core Ops, SparseCore 0:
  19.1 122.8 all-reduce.1
  279.9 30.1 reduce-scatter.1
where the time goes:
time: 320 us; the launch traced here: 319 us
  waiting for transfers between devices  148 us (46%)
  blocking collectives  94.5 us (30%)
  other arithmetic  29.3 us (9%)
  matrix products  28.4 us (9%)
  between operations  13.7 us (4%)
  local copies, waits for them, and re-layouts  4.93 us (2%)
    psum x1, waiting for transfers between devices, shards(): core_matrix = lax.psum(partial_core, ('src', 'tgt')) / total_pairs  117 us
    all_gather x8, blocking collectives, joined(): pieces = jax.tree.map(lambda part: lax.all_gather(part, axis), value)  94.5 us
    reduce_scatter x1, waiting for transfers between devices, shards(): lax.psum_scatter(jnp.dot(weights, target_genes, preferred_element_type=jn...  30.3 us
    dot_general x1, matrix products, shards(): lax.dot_general(left_src, geometry_right, (((0,), (0,)), ((), ())), preci...  11.4 us
    reduce_max x2, other arithmetic, row_logsum(): local_max = jnp.max(scores, axis=1)  8.87 us
    reduce_sum x2, other arithmetic, row_logsum(): local_sum = jnp.sum(jnp.exp(scores - local_max[:, None]), axis=1)  7.28 us
  transfers between devices with their start and end apart: 2, of which 2 were waited for; matrix products, arithmetic and copies ran while one was open for 2% of the time, Pallas kernels for 0%

commit v1 on v0

v1 whole, which is shorter than its diff:
```python
import functools
import math

import jax
import jax.numpy as jnp
from jax import lax
from jax.experimental import pallas as pl
from jax.experimental.pallas import tpu as pltpu
from jax.sharding import PartitionSpec as P

EPSILON = 0.05
GEOMETRY_WEIGHT = 4.0
LOG2E = math.log2(math.e)
KAPPA = 2.0 * LOG2E / EPSILON
MESH = pl.DeviceIdType.MESH
F32 = jnp.float32
BF16 = jnp.bfloat16
TILES = 17
HIGHEST = lax.Precision.HIGHEST


def split3(value):
    high = value.astype(BF16)
    rest = value - high.astype(F32)
    middle = rest.astype(BF16)
    low = (rest - middle.astype(F32)).astype(BF16)
    return high, middle, low


def dot(a, b, dims):
    return lax.dot_general(a, b, (dims, ((), ())), preferred_element_type=F32)


def dot3(a, b, dims):
    high, middle, low = split3(a)
    return dot(high, b, dims) + (dot(middle, b, dims) + dot(low, b, dims))


def exact(a, b, dims):
    return lax.dot_general(a, b, (dims, ((), ())), precision=HIGHEST, preferred_element_type=F32)


def kernel(
    src_n, tgt_n, total_pairs, rows, step,
    es_ref, et_ref, xs_ref, xt_ref, plan_ref, ms_ref, mt_ref, fs_ref, genes_ref,
    out_ref,
    right, xf, lhs_rest, emb, expr, tmass, genes, partial, collected, core,
    rhs, yf, score, lse, gpot, colmax, colsum,
    tgt_send, tgt_recv, rs_send, rs_recv, ag_send, ag_recv, lse_send, lse_recv,
):
    n = src_n * tgt_n
    s = lax.axis_index("src")
    t = lax.axis_index("tgt")
    me = s * tgt_n + t
    cols = et_ref.shape[1]
    nt = cols * tgt_n
    local = es_ref.shape[1]
    lanes = nt // 128
    base = t * rows

    def place(linear):
        return (linear // tgt_n, linear % tgt_n)

    def owner(tile):
        return (tile, tile % 2) if tile < 16 else (0, 1)

    barrier = pltpu.get_barrier_semaphore()

    def greet(k, carry):
        pl.semaphore_signal(barrier, inc=1, device_id=place((me + k) % n), device_id_type=MESH)
        return carry

    lax.fori_loop(1, n, greet, 0)

    embed = es_ref[...]
    right[0:128, :] = embed
    wide = embed.astype(F32)
    q_src = jnp.sum(wide * wide, axis=0, keepdims=True)
    xf[...] = jnp.zeros_like(xf)
    xf[0:3, :] = jnp.ones((3, local), F32)

    def put(ref, value, spots):
        pieces = split3(value)
        for piece, places in zip(pieces, spots):
            for at in places:
                ref[at:at + 1, :] = piece.astype(F32)

    put(xf, q_src, ((3, 4, 5), (6, 7), (8,)))
    put(xf, 0.5 * fs_ref[...], ((9,), (10,), (11,)))
    put(xf, jnp.log2(ms_ref[...]), ((12,), (13,), (14,)))
    put(xf, ms_ref[...], ((15,), (16,), (17,)))
    right[128:160, :] = xf[...].astype(BF16)

    pl.semaphore_wait(barrier, n - 1)

    sent = []
    for d in range(1, tgt_n):
        peer = (s, (t + d) % tgt_n)
        for a, (ref, place_ref) in enumerate(
            ((et_ref, emb), (xt_ref, expr), (mt_ref, tmass), (genes_ref, genes))
        ):
            sent.append(
                pltpu.make_async_remote_copy(
                    src_ref=ref, dst_ref=place_ref.at[t],
                    send_sem=tgt_send.at[a, d - 1], recv_sem=tgt_recv.at[a, d - 1],
                    device_id=peer, device_id_type=MESH,
                )
            )
    for copy in sent:
        copy.start()
    emb[t] = et_ref[...]
    expr[t] = xt_ref[...]
    tmass[t] = mt_ref[...]
    genes[t] = genes_ref[...]

    here = dot(right[...], plan_ref[...], ((1,), (0,)))
    target = et_ref[...]
    target_wide = target.astype(F32)
    q_tgt = jnp.sum(target_wide * target_wide, axis=0, keepdims=True)
    by_e = here[0:128, :]
    by_one = here[128:129, :]
    by_q = here[131:132, :] + (here[134:135, :] + here[136:137, :])
    partial[0:16] = dot3(by_e, target, ((1,), (1,))).reshape(16, 8, 128)
    row = lax.broadcasted_iota(jnp.int32, (8, cols), 0)
    pair = jnp.where(row == 0, 1.0, jnp.where(row == 1, q_tgt, 0.0))
    sums = jnp.where(row == 2, by_one, jnp.where(row == 3, by_q, 0.0))
    border = exact(pair, by_e, ((1,), (1,))) + dot3(sums, target, ((1,), (1,)))
    scalar_rows = jnp.where(
        row == 4, by_one,
        jnp.where(row == 5, by_one * q_tgt, jnp.where(row == 6, by_q, jnp.where(row == 7, by_q * q_tgt, 0.0))),
    )
    border = border + jnp.sum(scalar_rows, axis=1, keepdims=True)
    partial[16] = border

    def to_owner(tile):
        return pltpu.make_async_remote_copy(
            src_ref=partial.at[tile], dst_ref=collected.at[me],
            send_sem=rs_send.at[tile], recv_sem=rs_recv,
            device_id=owner(tile), device_id_type=MESH,
        )

    def mine(tile):
        return (s == owner(tile)[0]) & (t == owner(tile)[1])

    for tile in range(TILES):
        @pl.when(jnp.logical_not(mine(tile)))
        def _():
            to_owner(tile).start()

    own_tile = jnp.where((s == 0) & (t == 1), 16, jnp.minimum(s, 15))
    owns = ((s < 16) & (t == s % 2)) | ((s == 0) & (t == 1))

    @pl.when(owns)
    def _():
        collected[me] = partial[own_tile]
        whole = collected.at[pl.ds(0, n - 1)]
        pltpu.make_async_remote_copy(
            src_ref=whole, dst_ref=whole, send_sem=ag_send, recv_sem=rs_recv,
            device_id=place((me + 1) % n), device_id_type=MESH,
        ).wait_recv()
        core[own_tile] = jnp.sum(collected[...], axis=0)

        def spread(k, carry):
            pltpu.make_async_remote_copy(
                src_ref=core.at[own_tile], dst_ref=core.at[own_tile],
                send_sem=ag_send, recv_sem=ag_recv.at[own_tile],
                device_id=place((me + k) % n), device_id_type=MESH,
            ).start()
            return carry

        lax.fori_loop(1, n, spread, 0)

    for copy in sent[0::4] + sent[1::4] + sent[2::4]:
        copy.wait_recv()

    for tile in range(TILES):
        @pl.when(jnp.logical_not(mine(tile)))
        def _():
            pltpu.make_async_remote_copy(
                src_ref=core.at[tile], dst_ref=core.at[tile],
                send_sem=ag_send, recv_sem=ag_recv.at[tile],
                device_id=place((me + 1) % n), device_id_type=MESH,
            ).wait_recv()

    middle = core[0:16].reshape(128, 128) / total_pairs
    edge = core[16] / total_pairs
    yf[...] = jnp.zeros_like(yf)
    yf[9:12, :] = jnp.ones((3, nt), F32)
    row8 = lax.broadcasted_iota(jnp.int32, (8, cols), 0)
    for block in range(tgt_n):
        at = slice(block * cols, (block + 1) * cols)
        e_t = emb[block]
        e_wide = e_t.astype(F32)
        q_t = jnp.sum(e_wide * e_wide, axis=0, keepdims=True)
        ends = jnp.where(row8 == 0, q_t, jnp.where(row8 == 1, 1.0, 0.0))
        g_e = -2.0 * dot3(middle, e_t, ((1,), (0,))) + exact(edge, ends, ((0,), (0,)))
        high, mid, low = split3((-2.0 * GEOMETRY_WEIGHT) * g_e)
        rhs[0:128, at] = expr[block]
        rhs[128:256, at] = high
        rhs[256:384, at] = mid
        rhs[384:512, at] = low
        g_x = -2.0 * dot3(edge, e_t, ((1,), (0,)))
        g_0 = g_x[2:3, :] + edge[4:5, 0:1] * q_t + edge[5:6, 0:1]
        g_1 = g_x[3:4, :] + edge[6:7, 0:1] * q_t + edge[7:8, 0:1]
        high, mid, low = [p.astype(F32) for p in split3(GEOMETRY_WEIGHT * g_1)]
        yf[0:1, at] = high
        yf[1:2, at] = mid
        yf[2:3, at] = low
        high, mid, low = [p.astype(F32) for p in split3(GEOMETRY_WEIGHT * g_0)]
        for spot, piece in zip(range(3, 9), (high, mid, low, high, mid, high)):
            yf[spot:spot + 1, at] = piece
    rhs[512:544, :] = yf[...].astype(BF16)

    def column_fold(values):
        top = jnp.max(values, axis=0, keepdims=True)
        before = colmax[...]
        now = jnp.maximum(before, top)
        colsum[...] = colsum[...] * jnp.exp2(before - now) + jnp.sum(
            jnp.exp2(values - now), axis=0, keepdims=True
        )
        colmax[...] = now

    def column_start():
        colmax[...] = jnp.full_like(colmax, -1e30)
        colsum[...] = jnp.zeros_like(colsum)

    def share(turn):
        held = colmax[...] + jnp.log2(colsum[...])
        for c in range(lanes):
            lse[turn, me, c:c + 1, :] = held[:, c * 128:(c + 1) * 128]

        def spread(k, carry):
            pltpu.make_async_remote_copy(
                src_ref=lse.at[turn, me], dst_ref=lse.at[turn, me],
                send_sem=lse_send.at[turn], recv_sem=lse_recv.at[turn],
                device_id=place((me + k) % n), device_id_type=MESH,
            ).start()
            return carry

        lax.fori_loop(1, n, spread, 0)
        whole = lse.at[turn, pl.ds(0, n - 1)]
        every = pltpu.make_async_remote_copy(
            src_ref=whole, dst_ref=whole,
            send_sem=lse_send.at[turn], recv_sem=lse_recv.at[turn],
            device_id=place((me + 1) % n), device_id_type=MESH,
        )
        every.wait_recv()
        parts = lse[turn]
        top = jnp.max(parts, axis=0)
        total = jnp.sum(jnp.exp2(parts - top[None]), axis=0)
        value = jnp.log2(tmass[...].reshape(lanes, 128)) - (top + jnp.log2(total))
        for c in range(lanes):
            gpot[0:1, c * 128:(c + 1) * 128] = value[c:c + 1, :]
        return every

    column_start()

    def scores(c, carry):
        src = pl.ds(pl.multiple_of(base + c * step, 128), step)
        e_s = right[0:128, src]
        a = jnp.concatenate([xs_ref[:, src], e_s], axis=0)
        b = jnp.concatenate([e_s, e_s], axis=0)
        tile = dot(a, rhs[0:256, :], ((0,), (0,)))
        tile = tile + dot(b, rhs[256:512, :], ((0,), (0,)))
        tile = tile + dot(right[128:160, src], rhs[512:544, :], ((0,), (0,)))
        tile = tile * KAPPA
        score[pl.ds(pl.multiple_of(c * step, 128), step), :] = tile
        column_fold(tile)
        return carry

    lax.fori_loop(0, rows // step, scores, 0)
    first = share(0)

    pick = lax.broadcasted_iota(jnp.int32, (32, 256), 0)
    side = lax.broadcasted_iota(jnp.int32, (32, 256), 1) // 128
    select = jnp.where(
        (pick >= 12 + 3 * side) & (pick < 15 + 3 * side), 1.0, 0.0
    ).astype(BF16)

    def source_columns(c):
        src = pl.ds(pl.multiple_of(base + c * step, 128), step)
        both = dot(right[128:160, src], select, ((0,), (0,)))
        return both[:, 0:1], both[:, 128:129]

    column_start()

    def middle_pass(c, carry):
        tile = score[pl.ds(pl.multiple_of(c * step, 128), step), :]
        log_mass, unused = source_columns(c)
        a = tile + gpot[...]
        top = jnp.max(a, axis=1, keepdims=True)
        total = jnp.sum(jnp.exp2(a - top), axis=1, keepdims=True)
        moved = log_mass - (top + jnp.log2(total))
        column_fold(tile + moved)
        return carry

    lax.fori_loop(0, rows // step, middle_pass, 0)
    second = share(1)

    for copy in sent[3::4]:
        copy.wait_recv()
    gene_rows = genes[...].reshape(nt, genes.shape[2])

    def last_pass(c, carry):
        at = pl.ds(pl.multiple_of(c * step, 128), step)
        log_mass, mass = source_columns(c)
        a = score[at, :] + gpot[...]
        top = jnp.max(a, axis=1, keepdims=True)
        p = jnp.exp2(a - top)
        total = jnp.sum(p, axis=1, keepdims=True)
        potential = log_mass - (top + jnp.log2(total))
        numerator = dot(p.astype(BF16), gene_rows, ((1,), (0,)))
        out_ref[at, :] = (numerator * (jnp.exp2(potential + top) / mass)).astype(BF16)
        return carry

    lax.fori_loop(0, rows // step, last_pass, 0)

    for copy in sent:
        copy.wait_send()
    for tile in range(TILES):
        @pl.when(jnp.logical_not(mine(tile)))
        def _():
            to_owner(tile).wait_send()

    @pl.when(owns)
    def _():
        whole = collected.at[pl.ds(0, n - 1)]
        pltpu.make_async_remote_copy(
            src_ref=whole, dst_ref=whole, send_sem=ag_send, recv_sem=rs_recv,
            device_id=place((me + 1) % n), device_id_type=MESH,
        ).wait_send()

    first.wait_send()
    second.wait_send()


def shards(src_n, tgt_n, es, et, xs, xt, plan, ms, mt, fs, genes):
    n = src_n * tgt_n
    local = es.shape[1]
    cols = et.shape[1]
    nt = cols * tgt_n
    rows = local // tgt_n
    step = min(rows, 256) if nt <= 1024 else 128
    total_pairs = float(local * src_n * nt)
    gene_count = genes.shape[1]
    body = functools.partial(kernel, src_n, tgt_n, total_pairs, rows, step)
    vmem = pl.BlockSpec(memory_space=pltpu.VMEM)
    dma = pltpu.SemaphoreType.DMA
    return pl.pallas_call(
        body,
        out_shape=jax.ShapeDtypeStruct((rows, gene_count), BF16),
        in_specs=[vmem] * 9,
        out_specs=vmem,
        scratch_shapes=[
            pltpu.VMEM((160, local), BF16),
            pltpu.VMEM((32, local), F32),
            pltpu.VMEM((8, 128), F32),
            pltpu.VMEM((tgt_n, 128, cols), BF16),
            pltpu.VMEM((tgt_n, 128, cols), BF16),
            pltpu.VMEM((tgt_n, cols // 128, 128), F32),
            pltpu.VMEM((tgt_n, cols, gene_count), BF16),
            pltpu.VMEM((TILES, 8, 128), F32),
            pltpu.VMEM((n, 8, 128), F32),
            pltpu.VMEM((TILES, 8, 128), F32),
            pltpu.VMEM((544, nt), BF16),
            pltpu.VMEM((32, nt), F32),
            pltpu.VMEM((rows, nt), F32),
            pltpu.VMEM((2, n, nt // 128, 128), F32),
            pltpu.VMEM((1, nt), F32),
            pltpu.VMEM((1, nt), F32),
            pltpu.VMEM((1, nt), F32),
            dma((4, tgt_n - 1)),
            dma((4, tgt_n - 1)),
            dma((TILES,)),
            dma,
            dma,
            dma((TILES,)),
            dma((2,)),
            dma((2,)),
        ],
        compiler_params=pltpu.CompilerParams(
            collective_id=0, has_side_effects=True, vmem_limit_bytes=56 * 1024 * 1024
        ),
    )(
        es, et, xs, xt, plan,
        ms.reshape(1, local), mt.reshape(cols // 128, 128), fs.reshape(1, local), genes,
    )


def solution(mesh):
    src_n = mesh.shape["src"]
    tgt_n = mesh.shape["tgt"]
    return jax.shard_map(
        functools.partial(shards, src_n, tgt_n),
        mesh=mesh,
        in_specs=(
            P(None, "src"),
            P(None, "tgt"),
            P(None, "src"),
            P(None, "tgt"),
            P("src", "tgt"),
            P("src"),
            P("tgt"),
            P("src"),
            P("tgt", None),
        ),
        out_specs=P(("src", "tgt"), None),
        check_vma=False,
    )
```

time: 320 us -> 60.7 us (0.19)
  waiting for transfers between devices: 148 us -> 0 us
  blocking collectives: 94.5 us -> 0 us
  Pallas kernels: 0 us -> 58.3 us
  other arithmetic: 29.3 us -> 0 us
  matrix products: 28.4 us -> 0 us
  between operations: 13.7 us -> 0.01 us
    psum x1 -> x0, waiting for transfers between devices: 117 us -> none  [shards(): core_matrix = lax.psum(partial_core, ('src', 'tgt')) / total_pairs]
    all_gather x8 -> x0, blocking collectives: 94.5 us -> none  [joined(): pieces = jax.tree.map(lambda part: lax.all_gather(part, axis), value)]
    pallas_call x0 -> x1, Pallas kernels: none -> 58.3 us  [shards(): pl.pallas_call(body, out_shape=jax.ShapeDtypeStruct((rows, gene_count), B...]
    reduce_scatter x1 -> x0, waiting for transfers between devices: 30.3 us -> none  [shards(): lax.psum_scatter(jnp.dot(weights, target_genes, preferred_element_type=jn...]
    dot_general x6 -> x0, matrix products: 28.4 us -> none  [the longest x1 11.4 us: shards(): lax.dot_general(left_src, geometry_right, (((0,), (0,)), ((), ())), preci...]
    reduce_sum x5 -> x0, other arithmetic: 12 us -> none  [the longest x2 7.28 us: row_logsum(): local_sum = jnp.sum(jnp.exp(scores - local_max[:, None]), axis=1)]
    reduce_max x3 -> x0, other arithmetic: 9.85 us -> none  [the longest x2 8.87 us: row_logsum(): local_max = jnp.max(scores, axis=1)]
    convert_element_type x3 -> x0, other arithmetic: 5.19 us -> none  [the longest x2 2.65 us: factors(): widened = embed.astype(jnp.float32)]
  transfers between devices with their start and end apart: 2 -> 0, of which waited for: 2 -> 0; matrix products, arithmetic and copies ran while one was open for 2% -> 0% of each run, Pallas kernels for 0% -> 0%
where the time goes in v1:
time: 60.7 us; the launch traced here: 60.6 us
  Pallas kernels  58.3 us (96%)
  local copies, waits for them, and re-layouts  2.26 us (4%)
    pallas_call x1, Pallas kernels, shards(): pl.pallas_call(body, out_shape=jax.ShapeDtypeStruct((rows, gene_count), B...  58.3 us
    unnamed x1, local copies, waits for them, and re-layouts  2.26 us

profile of v1, /device:TPU:0, one launch (start us, length us, event | category | flops | bytes accessed | tf_op | source)
XLA Modules:
  0.0 60.6 jit_solution(12666023471196279811)
XLA Ops:
  0.0 58.3 %shard_map.91 = bf16[2048,256]{1,0:T(8,128)(2,1)} custom-call(bf16[128,4096]{1,0:T(8,128)(2,1)} %es_ref.1, bf16[128,512]{1,0:T(8,128)(2,1)} %et_ref.1, bf16[128,4096]{1,0:T(8,128)(2,1)} %xs_ref.1, bf16[128,512]{1,0:T(8,128)(2,1)} %xt_ref.1, bf16[4096,512]{1,0:T(8,128)(2,1)} %plan_ref.1, f32[1,4096]{1,0:T(1,128)} %bitcast.3, f32[4,128]{1,0:T(4,128)} %bitcast.5, ...), custom_call_target="tpu_custom_call" | custom-call | tf_op jit(solution)/shard_map/pallas_call | solution.py:349
  58.3 2.3 %copy.11 = bf16[2048,256]{1,0:T(8,128)(2,1)} copy(bf16[2048,256]{1,0:T(8,128)(2,1)} %shard_map.91) | data formatting | bytes 2097152

commit v2 on v1

--- a/solution.py
+++ b/solution.py
@@ -16,6 +16,7 @@
 F32 = jnp.float32
 BF16 = jnp.bfloat16
 TILES = 17
+CHUNKS = 4
 HIGHEST = lax.Precision.HIGHEST
 
 
@@ -44,9 +45,10 @@
     src_n, tgt_n, total_pairs, rows, step,
     es_ref, et_ref, xs_ref, xt_ref, plan_ref, ms_ref, mt_ref, fs_ref, genes_ref,
     out_ref,
-    right, xf, lhs_rest, emb, expr, tmass, genes, partial, collected, core,
-    rhs, yf, score, lse, gpot, colmax, colsum,
-    tgt_send, tgt_recv, rs_send, rs_recv, ag_send, ag_recv, lse_send, lse_recv,
+    right, xf, plan, xs, emb, expr, tmass, genes, partial, collected, core,
+    rhs, yf, score, near, far, gpot, colmax, colsum,
+    in_sem, tgt_send, tgt_recv, fw_send, fw_recv, rs_send, rs_recv, ag_send, ag_recv,
+    near_send, near_recv, far_send, far_recv,
 ):
     n = src_n * tgt_n
     s = lax.axis_index("src")
@@ -72,9 +74,24 @@
 
     lax.fori_loop(1, n, greet, 0)
 
-    embed = es_ref[...]
-    right[0:128, :] = embed
-    wide = embed.astype(F32)
+    plan_step = local // CHUNKS
+    fetch_embed = pltpu.make_async_copy(es_ref, right.at[0:128], in_sem.at[0])
+    fetch_plan = [
+        pltpu.make_async_copy(
+            plan_ref.at[c * plan_step:(c + 1) * plan_step],
+            plan.at[c * plan_step:(c + 1) * plan_step], in_sem.at[3 + c],
+        )
+        for c in range(CHUNKS)
+    ]
+    fetch_expr = pltpu.make_async_copy(
+        xs_ref.at[:, pl.ds(pl.multiple_of(base, 128), rows)], xs, in_sem.at[1]
+    )
+    fetch_genes = pltpu.make_async_copy(genes_ref, genes.at[t], in_sem.at[2])
+    for copy in [fetch_embed] + fetch_plan + [fetch_expr, fetch_genes]:
+        copy.start()
+    fetch_embed.wait()
+
+    wide = right[0:128, :].astype(F32)
     q_src = jnp.sum(wide * wide, axis=0, keepdims=True)
     xf[...] = jnp.zeros_like(xf)
     xf[0:3, :] = jnp.ones((3, local), F32)
@@ -93,27 +110,53 @@
 
     pl.semaphore_wait(barrier, n - 1)
 
-    sent = []
+    half = s % 2
+    sibling = (s + 1 - 2 * half, t)
+
+    def part(size):
+        return pl.ds(pl.multiple_of(half * (size // 2), size // 2), size // 2)
+
+    emb_part, gene_part = part(128), part(cols)
+    across, along = [], []
     for d in range(1, tgt_n):
         peer = (s, (t + d) % tgt_n)
-        for a, (ref, place_ref) in enumerate(
-            ((et_ref, emb), (xt_ref, expr), (mt_ref, tmass), (genes_ref, genes))
+        other = (t + tgt_n - d) % tgt_n
+        for a, (ref, held, piece) in enumerate(
+            ((et_ref, emb, emb_part), (xt_ref, expr, emb_part), (genes.at[t], genes, gene_part))
         ):
-            sent.append(
+            across.append(
                 pltpu.make_async_remote_copy(
-                    src_ref=ref, dst_ref=place_ref.at[t],
+                    src_ref=ref.at[piece], dst_ref=held.at[t, piece],
                     send_sem=tgt_send.at[a, d - 1], recv_sem=tgt_recv.at[a, d - 1],
                     device_id=peer, device_id_type=MESH,
                 )
             )
-    for copy in sent:
+            along.append(
+                pltpu.make_async_remote_copy(
+                    src_ref=held.at[other, piece], dst_ref=held.at[other, piece],
+                    send_sem=fw_send.at[a, d - 1], recv_sem=fw_recv.at[a, d - 1],
+                    device_id=sibling, device_id_type=MESH,
+                )
+            )
+    masses = [
+        pltpu.make_async_remote_copy(
+            src_ref=mt_ref, dst_ref=tmass.at[t],
+            send_sem=tgt_send.at[3, d - 1], recv_sem=tgt_recv.at[3, d - 1],
+            device_id=(s, (t + d) % tgt_n), device_id_type=MESH,
+        )
+        for d in range(1, tgt_n)
+    ]
+    for copy in across[0::3] + across[1::3] + masses:
         copy.start()
     emb[t] = et_ref[...]
     expr[t] = xt_ref[...]
     tmass[t] = mt_ref[...]
-    genes[t] = genes_ref[...]
-
-    here = dot(right[...], plan_ref[...], ((1,), (0,)))
+
+    here = 0.0
+    for c in range(CHUNKS):
+        fetch_plan[c].wait()
+        at = slice(c * plan_step, (c + 1) * plan_step)
+        here = here + dot(right[:, at], plan[at, :], ((1,), (0,)))
     target = et_ref[...]
     target_wide = target.astype(F32)
     q_tgt = jnp.sum(target_wide * target_wide, axis=0, keepdims=True)
@@ -147,6 +190,10 @@
         def _():
             to_owner(tile).start()
 
+    for copy, onward in list(zip(across, along))[0::3] + list(zip(across, along))[1::3]:
+        copy.wait_recv()
+        onward.start()
+
     own_tile = jnp.where((s == 0) & (t == 1), 16, jnp.minimum(s, 15))
     owns = ((s < 16) & (t == s % 2)) | ((s == 0) & (t == 1))
 
@@ -170,7 +217,7 @@
 
         lax.fori_loop(1, n, spread, 0)
 
-    for copy in sent[0::4] + sent[1::4] + sent[2::4]:
+    for copy in along[0::3] + along[1::3] + masses:
         copy.wait_recv()
 
     for tile in range(TILES):
@@ -181,6 +228,10 @@
                 send_sem=ag_send, recv_sem=ag_recv.at[tile],
                 device_id=place((me + 1) % n), device_id_type=MESH,
             ).wait_recv()
+
+    fetch_genes.wait()
+    for copy in across[2::3]:
+        copy.start()
 
     middle = core[0:16].reshape(128, 128) / total_pairs
     edge = core[16] / total_pairs
@@ -224,41 +275,58 @@
         colmax[...] = jnp.full_like(colmax, -1e30)
         colsum[...] = jnp.zeros_like(colsum)
 
+    group = 4 * tgt_n
+    rank = me % group
+    level = me // group
+    first_near = level * group
+
+    def joined(parts):
+        top = jnp.max(parts, axis=0)
+        return top, jnp.sum(jnp.exp2(parts - top[None]), axis=0)
+
+    def exchange(slots, slot, count, send_sem, recv_sem, peer):
+        for k in range(1, count):
+            pltpu.make_async_remote_copy(
+                src_ref=slots.at[slot], dst_ref=slots.at[slot],
+                send_sem=send_sem, recv_sem=recv_sem,
+                device_id=peer(k), device_id_type=MESH,
+            ).start()
+        whole = slots.at[pl.ds(0, count - 1)]
+        every = pltpu.make_async_remote_copy(
+            src_ref=whole, dst_ref=whole, send_sem=send_sem, recv_sem=recv_sem,
+            device_id=peer(1), device_id_type=MESH,
+        )
+        every.wait_recv()
+        return every
+
     def share(turn):
         held = colmax[...] + jnp.log2(colsum[...])
         for c in range(lanes):
-            lse[turn, me, c:c + 1, :] = held[:, c * 128:(c + 1) * 128]
-
-        def spread(k, carry):
-            pltpu.make_async_remote_copy(
-                src_ref=lse.at[turn, me], dst_ref=lse.at[turn, me],
-                send_sem=lse_send.at[turn], recv_sem=lse_recv.at[turn],
-                device_id=place((me + k) % n), device_id_type=MESH,
-            ).start()
-            return carry
-
-        lax.fori_loop(1, n, spread, 0)
-        whole = lse.at[turn, pl.ds(0, n - 1)]
-        every = pltpu.make_async_remote_copy(
-            src_ref=whole, dst_ref=whole,
-            send_sem=lse_send.at[turn], recv_sem=lse_recv.at[turn],
-            device_id=place((me + 1) % n), device_id_type=MESH,
-        )
-        every.wait_recv()
-        parts = lse[turn]
-        top = jnp.max(parts, axis=0)
-        total = jnp.sum(jnp.exp2(parts - top[None]), axis=0)
+            near[turn, rank, c:c + 1, :] = held[:, c * 128:(c + 1) * 128]
+        close = exchange(
+            near.at[turn], rank, group, near_send.at[turn], near_recv.at[turn],
+            lambda k: place(first_near + (rank + k) % group),
+        )
+        top, total = joined(near[turn])
+        far[turn, level] = top + jnp.log2(total)
+        wide_range = exchange(
+            far.at[turn], level, n // group, far_send.at[turn], far_recv.at[turn],
+            lambda k: place((me + k * group) % n),
+        )
+        top, total = joined(far[turn])
         value = jnp.log2(tmass[...].reshape(lanes, 128)) - (top + jnp.log2(total))
         for c in range(lanes):
             gpot[0:1, c * 128:(c + 1) * 128] = value[c:c + 1, :]
-        return every
+        return close, wide_range
+
+    fetch_expr.wait()
 
     column_start()
 
     def scores(c, carry):
         src = pl.ds(pl.multiple_of(base + c * step, 128), step)
         e_s = right[0:128, src]
-        a = jnp.concatenate([xs_ref[:, src], e_s], axis=0)
+        a = jnp.concatenate([xs[:, pl.ds(pl.multiple_of(c * step, 128), step)], e_s], axis=0)
         b = jnp.concatenate([e_s, e_s], axis=0)
         tile = dot(a, rhs[0:256, :], ((0,), (0,)))
         tile = tile + dot(b, rhs[256:512, :], ((0,), (0,)))
@@ -270,6 +338,9 @@
 
     lax.fori_loop(0, rows // step, scores, 0)
     first = share(0)
+    for copy, onward in list(zip(across, along))[2::3]:
+        copy.wait_recv()
+        onward.start()
 
     pick = lax.broadcasted_iota(jnp.int32, (32, 256), 0)
     side = lax.broadcasted_iota(jnp.int32, (32, 256), 1) // 128
@@ -297,7 +368,7 @@
     lax.fori_loop(0, rows // step, middle_pass, 0)
     second = share(1)
 
-    for copy in sent[3::4]:
+    for copy in along[2::3]:
         copy.wait_recv()
     gene_rows = genes[...].reshape(nt, genes.shape[2])
 
@@ -315,7 +386,7 @@
 
     lax.fori_loop(0, rows // step, last_pass, 0)
 
-    for copy in sent:
+    for copy in across + along + masses + list(first) + list(second):
         copy.wait_send()
     for tile in range(TILES):
         @pl.when(jnp.logical_not(mine(tile)))
@@ -329,9 +400,6 @@
             src_ref=whole, dst_ref=whole, send_sem=ag_send, recv_sem=rs_recv,
             device_id=place((me + 1) % n), device_id_type=MESH,
         ).wait_send()
-
-    first.wait_send()
-    second.wait_send()
 
 
 def shards(src_n, tgt_n, es, et, xs, xt, plan, ms, mt, fs, genes):
@@ -344,17 +412,19 @@
     total_pairs = float(local * src_n * nt)
     gene_count = genes.shape[1]
     body = functools.partial(kernel, src_n, tgt_n, total_pairs, rows, step)
+    anywhere = pl.BlockSpec(memory_space=pl.ANY)
     vmem = pl.BlockSpec(memory_space=pltpu.VMEM)
     dma = pltpu.SemaphoreType.DMA
     return pl.pallas_call(
         body,
         out_shape=jax.ShapeDtypeStruct((rows, gene_count), BF16),
-        in_specs=[vmem] * 9,
+        in_specs=[anywhere, vmem, anywhere, vmem, anywhere, vmem, vmem, vmem, anywhere],
         out_specs=vmem,
         scratch_shapes=[
             pltpu.VMEM((160, local), BF16),
             pltpu.VMEM((32, local), F32),
-            pltpu.VMEM((8, 128), F32),
+            pltpu.VMEM((local, cols), BF16),
+            pltpu.VMEM((128, rows), BF16),
             pltpu.VMEM((tgt_n, 128, cols), BF16),
             pltpu.VMEM((tgt_n, 128, cols), BF16),
             pltpu.VMEM((tgt_n, cols // 128, 128), F32),
@@ -365,16 +435,22 @@
             pltpu.VMEM((544, nt), BF16),
             pltpu.VMEM((32, nt), F32),
             pltpu.VMEM((rows, nt), F32),
-            pltpu.VMEM((2, n, nt // 128, 128), F32),
+            pltpu.VMEM((2, 4 * tgt_n, nt // 128, 128), F32),
+            pltpu.VMEM((2, src_n // 4, nt // 128, 128), F32),
             pltpu.VMEM((1, nt), F32),
             pltpu.VMEM((1, nt), F32),
             pltpu.VMEM((1, nt), F32),
+            dma((3 + CHUNKS,)),
             dma((4, tgt_n - 1)),
             dma((4, tgt_n - 1)),
+            dma((3, tgt_n - 1)),
+            dma((3, tgt_n - 1)),
             dma((TILES,)),
             dma,
             dma,
             dma((TILES,)),
+            dma((2,)),
+            dma((2,)),
             dma((2,)),
             dma((2,)),
         ],

time: 60.7 us -> 53.1 us (0.87)
  Pallas kernels: 58.3 us -> 50.6 us
    pallas_call x1, Pallas kernels: 58.3 us -> 50.6 us  [shards(): pl.pallas_call(body, out_shape=jax.ShapeDtypeStruct((rows, gene_count), B...]
where the time goes in v2:
time: 53.1 us; the launch traced here: 52.9 us
  Pallas kernels  50.6 us (95%)
  local copies, waits for them, and re-layouts  2.26 us (4%)
    pallas_call x1, Pallas kernels, shards(): pl.pallas_call(body, out_shape=jax.ShapeDtypeStruct((rows, gene_count), B...  50.6 us
    unnamed x1, local copies, waits for them, and re-layouts  2.26 us

profile of v2, /device:TPU:0, one launch (start us, length us, event | category | flops | bytes accessed | tf_op | source)
XLA Modules:
  0.0 52.9 jit_solution(17841653441960435565)
XLA Ops:
  0.0 50.6 %shard_map.91 = bf16[2048,256]{1,0:T(8,128)(2,1)} custom-call(bf16[128,4096]{1,0:T(8,128)(2,1)} %es_ref.1, bf16[128,512]{1,0:T(8,128)(2,1)} %et_ref.1, bf16[128,4096]{1,0:T(8,128)(2,1)} %xs_ref.1, bf16[128,512]{1,0:T(8,128)(2,1)} %xt_ref.1, bf16[4096,512]{1,0:T(8,128)(2,1)} %plan_ref.1, f32[1,4096]{1,0:T(1,128)} %bitcast.3, f32[4,128]{1,0:T(4,128)} %bitcast.5, ...), custom_call_target="tpu_custom_call" | custom-call | tf_op jit(solution)/shard_map/pallas_call | solution.py:418
  50.6 2.3 %copy.11 = bf16[2048,256]{1,0:T(8,128)(2,1)} copy(bf16[2048,256]{1,0:T(8,128)(2,1)} %shard_map.91) | data formatting | bytes 2097152

commit v3 on v2

--- a/solution.py
+++ b/solution.py
@@ -336,7 +336,7 @@
         column_fold(tile)
         return carry
 
-    lax.fori_loop(0, rows // step, scores, 0)
+    lax.fori_loop(0, rows // step, scores, 0, unroll=2)
     first = share(0)
     for copy, onward in list(zip(across, along))[2::3]:
         copy.wait_recv()
@@ -365,7 +365,7 @@
         column_fold(tile + moved)
         return carry
 
-    lax.fori_loop(0, rows // step, middle_pass, 0)
+    lax.fori_loop(0, rows // step, middle_pass, 0, unroll=2)
     second = share(1)
 
     for copy in along[2::3]:
@@ -384,7 +384,7 @@
         out_ref[at, :] = (numerator * (jnp.exp2(potential + top) / mass)).astype(BF16)
         return carry
 
-    lax.fori_loop(0, rows // step, last_pass, 0)
+    lax.fori_loop(0, rows // step, last_pass, 0, unroll=2)
 
     for copy in across + along + masses + list(first) + list(second):
         copy.wait_send()
@@ -408,7 +408,7 @@
     cols = et.shape[1]
     nt = cols * tgt_n
     rows = local // tgt_n
-    step = min(rows, 256) if nt <= 1024 else 128
+    step = min(rows, 512) if nt <= 1024 else 128
     total_pairs = float(local * src_n * nt)
     gene_count = genes.shape[1]
     body = functools.partial(kernel, src_n, tgt_n, total_pairs, rows, step)

time: 53.1 us -> 49.3 us (0.928)
  Pallas kernels: 50.6 us -> 46.9 us
    pallas_call x1, Pallas kernels: 50.6 us -> 46.9 us  [shards(): pl.pallas_call(body, out_shape=jax.ShapeDtypeStruct((rows, gene_count), B...]
where the time goes in v3:
time: 49.3 us; the launch traced here: 49.1 us
  Pallas kernels  46.9 us (95%)
  local copies, waits for them, and re-layouts  2.26 us (5%)
    pallas_call x1, Pallas kernels, shards(): pl.pallas_call(body, out_shape=jax.ShapeDtypeStruct((rows, gene_count), B...  46.9 us
    unnamed x1, local copies, waits for them, and re-layouts  2.26 us

profile of v3, /device:TPU:0, one launch (start us, length us, event | category | flops | bytes accessed | tf_op | source)
XLA Modules:
  0.0 49.1 jit_solution(14558371418658513023)
XLA Ops:
  0.0 46.9 %shard_map.91 = bf16[2048,256]{1,0:T(8,128)(2,1)} custom-call(bf16[128,4096]{1,0:T(8,128)(2,1)} %es_ref.1, bf16[128,512]{1,0:T(8,128)(2,1)} %et_ref.1, bf16[128,4096]{1,0:T(8,128)(2,1)} %xs_ref.1, bf16[128,512]{1,0:T(8,128)(2,1)} %xt_ref.1, bf16[4096,512]{1,0:T(8,128)(2,1)} %plan_ref.1, f32[1,4096]{1,0:T(1,128)} %bitcast.3, f32[4,128]{1,0:T(4,128)} %bitcast.5, ...), custom_call_target="tpu_custom_call" | custom-call | tf_op jit(solution)/shard_map/pallas_call | solution.py:418
  46.9 2.3 %copy.11 = bf16[2048,256]{1,0:T(8,128)(2,1)} copy(bf16[2048,256]{1,0:T(8,128)(2,1)} %shard_map.91) | data formatting | bytes 2097152

commit v4 on v3

--- a/solution.py
+++ b/solution.py
@@ -336,7 +336,7 @@
         column_fold(tile)
         return carry
 
-    lax.fori_loop(0, rows // step, scores, 0, unroll=2)
+    lax.fori_loop(0, rows // step, scores, 0, unroll=4)
     first = share(0)
     for copy, onward in list(zip(across, along))[2::3]:
         copy.wait_recv()
@@ -365,7 +365,7 @@
         column_fold(tile + moved)
         return carry
 
-    lax.fori_loop(0, rows // step, middle_pass, 0, unroll=2)
+    lax.fori_loop(0, rows // step, middle_pass, 0, unroll=4)
     second = share(1)
 
     for copy in along[2::3]:
@@ -384,7 +384,7 @@
         out_ref[at, :] = (numerator * (jnp.exp2(potential + top) / mass)).astype(BF16)
         return carry
 
-    lax.fori_loop(0, rows // step, last_pass, 0, unroll=2)
+    lax.fori_loop(0, rows // step, last_pass, 0, unroll=4)
 
     for copy in across + along + masses + list(first) + list(second):
         copy.wait_send()

time: 49.3 us -> 49.3 us (level)
  no operation moved by 1% of the time
where the time goes in v4:
time: 49.3 us; the launch traced here: 49.1 us
  Pallas kernels  46.9 us (95%)
  local copies, waits for them, and re-layouts  2.26 us (5%)
    pallas_call x1, Pallas kernels, shards(): pl.pallas_call(body, out_shape=jax.ShapeDtypeStruct((rows, gene_count), B...  46.9 us
    unnamed x1, local copies, waits for them, and re-layouts  2.26 us

profile of v4, /device:TPU:0, one launch (start us, length us, event | category | flops | bytes accessed | tf_op | source)
XLA Modules:
  0.0 49.1 jit_solution(17037894415295330037)
XLA Ops:
  0.0 46.9 %shard_map.91 = bf16[2048,256]{1,0:T(8,128)(2,1)} custom-call(bf16[128,4096]{1,0:T(8,128)(2,1)} %es_ref.1, bf16[128,512]{1,0:T(8,128)(2,1)} %et_ref.1, bf16[128,4096]{1,0:T(8,128)(2,1)} %xs_ref.1, bf16[128,512]{1,0:T(8,128)(2,1)} %xt_ref.1, bf16[4096,512]{1,0:T(8,128)(2,1)} %plan_ref.1, f32[1,4096]{1,0:T(1,128)} %bitcast.3, f32[4,128]{1,0:T(4,128)} %bitcast.5, ...), custom_call_target="tpu_custom_call" | custom-call | tf_op jit(solution)/shard_map/pallas_call | solution.py:418
  46.9 2.3 %copy.11 = bf16[2048,256]{1,0:T(8,128)(2,1)} copy(bf16[2048,256]{1,0:T(8,128)(2,1)} %shard_map.91) | data formatting | bytes 2097152
